TPU v7x, 32 devices: a whole 2x2x4 slice. The times are simulated.
32 devices in a mesh: req: 16 (over z, y, core), grp: 2 (over x).
Axes of the slice: x: 2, y: 2, z: 4, core: 2. Of those that a mesh axis runs over, the one named last changes fastest.
Arguments:
- tokens: bfloat16 [8192, 1024], P('req'), may hold values from -6 to 6
- norm_attn: float32 [1024], replicated, may hold values from 0.25 to 1.75
- w_query: bfloat16 [1024, 1024], P(None, 'grp'), may hold values from -0.1875 to 0.1875
- w_key: bfloat16 [1024, 1024], P(None, 'grp'), may hold values from -0.1875 to 0.1875
- w_value: bfloat16 [1024, 1024], P(None, 'grp'), may hold values from -0.1875 to 0.1875
- w_out: bfloat16 [1024, 1024], P('grp'), may hold values from -0.1875 to 0.1875
- persist_keys: bfloat16 [16, 1024], P(None, 'grp'), may hold values from -5 to 5
- persist_values: bfloat16 [16, 1024], P(None, 'grp'), may hold values from -5 to 5
- kv_cache: bfloat16 [768, 2, 128, 1024], P('req', None, None, 'grp'), may hold values from -160 to 160
- slot_request: int32 [768], P('req'), may hold values from 0 to 255, as said below
- slot_page: int32 [768], P('req'), may hold values from 0 to 48, as said below
- cache_len: int32 [256], P('req'), may hold values from 1 to 2304
- tree_mask: int32 [256, 32, 32], P('req'), may hold values from 0 to 1, as said below
- accept_path: int32 [256, 8], P('req'), may hold values from 0 to 31, as said below
- accept_len: int32 [256], P('req'), may hold values from 1 to 8
- memory: float32 [256, 8, 128, 128], P('req', 'grp'), may hold values from -4 to 4
- momentum: float32 [256, 8, 128, 128], P('req', 'grp'), may hold values from -1.2 to 1.2
- momentum_code: int32 [256, 8, 8], P('req', None, 'grp'), may hold values from 0 to 15
- forget_code: int32 [256, 8, 8], P('req', None, 'grp'), may hold values from 0 to 15
- norm_ffn: float32 [1024], replicated, may hold values from 0.25 to 1.75
- w_gate_up: bfloat16 [2, 1024, 2816], P(None, None, 'grp'), may hold values from -0.1875 to 0.1875
- w_down: bfloat16 [2816, 1024], P('grp'), may hold values from -0.109375 to 0.109375
Outputs:
- layer_out: bfloat16 [8192, 1024], P(('req', 'grp'))
- memory_out: float32 [256, 8, 128, 128], P('req', 'grp')
- momentum_out: float32 [256, 8, 128, 128], P('req', 'grp')
Inputs may be any that keep to these rules, and one draw needn't show every extreme that they name: `slot_request`: slot s lies with index s // 48 of req; slots s with (s % 48) // 3 = j hold pages of requests j * 16 to (j + 1) * 16 - 1 only. The live pages 0 .. ceil(cache_len[r] / 128) - 1 of every request stand each in exactly one slot; every other slot has page number 16 * 3. `slot_page`: see slot_request. `tree_mask`: each node's parent precedes it; node 0 is the root; rows include the node itself. `accept_path`: entry n is the node at depth n on the root path of one draft node.
All inputs are finite; a program needn't handle non-finite values.
Results may differ from a plain program's by a relative error of at most 0.015.
Values may be sent and summed in bfloat16 or wider, within the bound.
No kernel may reach another device: no remote copies, remote signals or barrier semaphores. Data moves between devices by JAX's collectives and lax.ppermute only.
A program may use at most 192 MiB of HBM per device.

v0:
```python
import math
import jax
import jax.numpy as jnp
from jax import lax
from jax.sharding import PartitionSpec as P

HD = 128
EPS = 1e-06
THETA = 0.5
NEG = -1e30


def rms_norm(rows, gain):
    values = rows.astype(jnp.float32)
    factor = lax.rsqrt(jnp.mean(values * values, axis=-1, keepdims=True) + EPS)
    return (values * factor * gain).astype(jnp.bfloat16)


def unit_rows(vectors):
    return vectors * lax.rsqrt(jnp.sum(vectors * vectors, axis=-1, keepdims=True) + EPS)


def page_partials(pages, page_queries, page_first, page_limit, scale):
    count = pages.shape[0]
    page_len = pages.shape[2]
    width = pages.shape[3]
    heads = width // HD
    draft = page_queries.shape[1]
    query_four = page_queries.reshape(count, draft, heads, HD)
    key_four = pages[:, 0].reshape(count, page_len, heads, HD)
    value_four = pages[:, 1].reshape(count, page_len, heads, HD)
    scores = (
        jnp.einsum("sihd,sthd->shit", query_four, key_four, preferred_element_type=jnp.float32)
        * scale
    )
    position = page_first[:, None] + jnp.arange(page_len, dtype=jnp.int32)[None, :]
    valid = (position < page_limit[:, None])[:, None, None, :]
    masked = jnp.where(valid, scores, NEG)
    top = jnp.max(masked, axis=3)
    weight = jnp.where(valid, jnp.exp(masked - top[..., None]), 0.0)
    total = jnp.sum(weight, axis=3)
    numer = jnp.einsum(
        "shit,sthd->sihd",
        weight.astype(jnp.bfloat16),
        value_four,
        preferred_element_type=jnp.float32,
    )
    return (numer.reshape(count, draft, width), top, total)


def on_device(
    tokens,
    norm_attn,
    w_query,
    w_key,
    w_value,
    w_out,
    persist_keys,
    persist_values,
    kv_cache,
    slot_request,
    slot_page,
    cache_len,
    tree_mask,
    accept_path,
    accept_len,
    memory,
    momentum,
    momentum_code,
    forget_code,
    norm_ffn,
    w_gate_up,
    w_down,
):
    group_rows = tokens.shape[0]
    reqs = cache_len.shape[0]
    draft = tree_mask.shape[1]
    width = w_query.shape[1]
    heads = width // HD
    fixed_count = persist_keys.shape[0]
    page_len = kv_cache.shape[2]
    scale = 1.0 / math.sqrt(HD)
    normed = rms_norm(tokens, norm_attn)
    queries = jnp.dot(normed, w_query, preferred_element_type=jnp.float32).astype(jnp.bfloat16)
    keys = jnp.dot(normed, w_key, preferred_element_type=jnp.float32).astype(jnp.bfloat16)
    values = jnp.dot(normed, w_value, preferred_element_type=jnp.float32).astype(jnp.bfloat16)
    query_four = queries.reshape(reqs, draft, heads, HD)
    key_four = keys.reshape(reqs, draft, heads, HD)
    value_four = values.reshape(reqs, draft, heads, HD)
    fixed_keys = persist_keys.reshape(fixed_count, heads, HD)
    fixed_values = persist_values.reshape(fixed_count, heads, HD)
    tree_scores = (
        jnp.einsum("rihd,rjhd->rhij", query_four, key_four, preferred_element_type=jnp.float32)
        * scale
    )
    tree_scores = jnp.where(tree_mask[:, None] == 1, tree_scores, NEG)
    fixed_scores = (
        jnp.einsum("rihd,phd->rhip", query_four, fixed_keys, preferred_element_type=jnp.float32)
        * scale
    )
    local_scores = jnp.concatenate([fixed_scores, tree_scores], axis=3)
    local_top = jnp.max(local_scores, axis=3)
    local_weight = jnp.exp(local_scores - local_top[..., None])
    local_total = jnp.sum(local_weight, axis=3)
    local_rounded = local_weight.astype(jnp.bfloat16)
    local_numer = jnp.einsum(
        "rhip,phd->rihd",
        local_rounded[..., :fixed_count],
        fixed_values,
        preferred_element_type=jnp.float32,
    )
    local_numer = local_numer + jnp.einsum(
        "rhij,rjhd->rihd",
        local_rounded[..., fixed_count:],
        value_four,
        preferred_element_type=jnp.float32,
    )
    first_request = lax.axis_index("req") * reqs
    request_ids = jnp.arange(reqs, dtype=jnp.int32)
    moved_pages, moved_request, moved_page = (
        lax.all_to_all(kv_cache, "req", split_axis=0, concat_axis=0, tiled=True),
        lax.all_to_all(slot_request, "req", split_axis=0, concat_axis=0, tiled=True),
        lax.all_to_all(slot_page, "req", split_axis=0, concat_axis=0, tiled=True),
    )
    local_request = moved_request - first_request
    pick = local_request[:, None] == request_ids[None, :]
    limits = jnp.sum(jnp.where(pick, cache_len[None, :], 0), axis=1)
    page_queries = queries.reshape(reqs, draft, width)[local_request]
    numer, top, total = page_partials(
        moved_pages, page_queries, moved_page * page_len, limits, scale
    )
    slot_count = numer.shape[0]
    pick_weight = pick.astype(jnp.float32)
    request_top = jnp.max(jnp.where(pick[:, :, None, None], top[:, None], NEG), axis=0)
    best = jnp.maximum(request_top, local_top)
    slot_best = jnp.einsum("sr,rhi->shi", pick_weight, best, precision=lax.Precision.HIGHEST)
    factor = jnp.exp(top - slot_best)
    scaled = (
        numer.reshape(slot_count, draft, heads, HD) * jnp.transpose(factor, (0, 2, 1))[..., None]
    )
    page_numer = jnp.einsum("sr,sihd->rihd", pick_weight, scaled, precision=lax.Precision.HIGHEST)
    page_total = jnp.einsum(
        "sr,shi->rhi", pick_weight, total * factor, precision=lax.Precision.HIGHEST
    )
    local_factor = jnp.exp(local_top - best)
    numer_all = local_numer * jnp.transpose(local_factor, (0, 2, 1))[..., None] + page_numer
    total_all = local_total * local_factor + page_total
    attention = numer_all / jnp.transpose(total_all, (0, 2, 1))[..., None]
    unit_query = unit_rows(query_four.astype(jnp.float32))
    retrieved = jnp.einsum("rihd,rhde->rihe", unit_query, memory, precision=lax.Precision.HIGHEST)
    mixed = (attention + retrieved).reshape(group_rows, width).astype(jnp.bfloat16)
    rows = group_rows // lax.axis_size("grp")
    head_sum = lax.psum_scatter(
        jnp.dot(mixed, w_out, preferred_element_type=jnp.float32).astype(jnp.bfloat16),
        "grp",
        scatter_dimension=0,
        tiled=True,
    ).astype(jnp.float32)
    own_rows = lax.dynamic_slice_in_dim(tokens, lax.axis_index("grp") * rows, rows, 0)
    residual = (own_rows.astype(jnp.float32) + head_sum).astype(jnp.bfloat16)
    ffn_in = rms_norm(residual, norm_ffn)
    piece = lax.all_gather(ffn_in, "grp", axis=0, tiled=True)
    gate = jnp.dot(piece, w_gate_up[0], preferred_element_type=jnp.float32)
    up = jnp.dot(piece, w_gate_up[1], preferred_element_type=jnp.float32)
    hidden = (jax.nn.silu(gate) * up).astype(jnp.bfloat16)
    ffn_out = lax.psum_scatter(
        jnp.dot(hidden, w_down, preferred_element_type=jnp.float32).astype(jnp.bfloat16),
        "grp",
        scatter_dimension=0,
        tiled=True,
    ).astype(jnp.float32)
    layer_out = (residual.astype(jnp.float32) + ffn_out).astype(jnp.bfloat16)
    req_rows = request_ids[:, None]
    path_keys = unit_rows(key_four[req_rows, accept_path].astype(jnp.float32))
    path_values = value_four[req_rows, accept_path].astype(jnp.float32)
    eta = 0.97 - 0.06 * momentum_code.astype(jnp.float32)
    forget = 0.01 + 0.02 * forget_code.astype(jnp.float32)
    for step in range(accept_path.shape[1]):
        unit = path_keys[:, step]
        predicted = jnp.einsum("rhd,rhde->rhe", unit, memory, precision=lax.Precision.HIGHEST)
        grad = jnp.einsum(
            "rhd,rhe->rhde", unit, predicted - path_values[:, step], precision=lax.Precision.HIGHEST
        )
        new_mom = eta[:, step, :, None, None] * momentum - THETA * grad
        new_mem = (1.0 - forget[:, step, :, None, None]) * memory + new_mom
        live = (step < accept_len)[:, None, None, None]
        momentum = jnp.where(live, new_mom, momentum)
        memory = jnp.where(live, new_mem, memory)
    return (layer_out, memory, momentum)


def solution(mesh):
    return jax.shard_map(
        on_device,
        mesh=mesh,
        in_specs=(
            P("req", None),
            P(),
            P(None, "grp"),
            P(None, "grp"),
            P(None, "grp"),
            P("grp", None),
            P(None, "grp"),
            P(None, "grp"),
            P("req", None, None, "grp"),
            P("req"),
            P("req"),
            P("req"),
            P("req", None, None),
            P("req", None),
            P("req"),
            P("req", "grp", None, None),
            P("req", "grp", None, None),
            P("req", None, "grp"),
            P("req", None, "grp"),
            P(),
            P(None, None, "grp"),
            P("grp", None),
        ),
        out_specs=(
            P(("req", "grp"), None),
            P("req", "grp", None, None),
            P("req", "grp", None, None),
        ),
        check_vma=False,
    )
```

profile of v0, /device:TPU:0, one launch (start us, length us, event | category | flops | bytes accessed | tf_op | source)
XLA Modules:
  0.0 470.7 jit_solution(17253716148561162837)
XLA Ops:
  8.7 7.4 %all-to-all-start = ((s32[16,3,1]{1,2,0:T(1,128)}), s32[16,3,1]{1,2,0:T(1,128)S(1)}, u32[]{:S(2)}, u32[]{:S(2)}) async-start(s32[16,3,1]{1,2,0:T(1,128)} %bitcast.6), calls=%async_computation | async-start | bytes 16384 | tf_op jit(solution)/shard_map/all_to_all | solution.py:122
  17.4 5.0 %all-to-all-done = s32[16,3,1]{1,2,0:T(1,128)S(1)} async-done(((s32[16,3,1]{1,2,0:T(1,128)}), s32[16,3,1]{1,2,0:T(1,128)S(1)}, u32[]{:S(2)}, u32[]{:S(2)}) %all-to-all-start) | async-done | bytes 224 | tf_op jit(solution)/shard_map/all_to_all | solution.py:122
  25.9 16.7 %copy.234 = bf16[48,2,128,512]{2,3,1,0:T(8,128)(2,1)} copy(bf16[48,2,128,512]{3,2,1,0:T(8,128)(2,1)} %param.30) | data formatting | bytes 25165824 | tf_op args[8]
  43.2 6.0 %all-to-all-start.2 = ((bf16[48,2,128,512]{2,3,1,0:T(8,128)(2,1)}), bf16[48,2,128,512]{2,3,1,0:T(8,128)(2,1)}, u32[]{:S(2)}, u32[]{:S(2)}) async-start(bf16[48,2,128,512]{2,3,1,0:T(8,128)(2,1)} %copy.234), calls=%async_computation.2 | async-start | bytes 25165824 | tf_op jit(solution)/shard_map/all_to_all | solution.py:121
  94.5 5.5 %fusion.145 = f32[16,4,1,128]{3,2,1,0:T(1,128)S(1)} fusion(f32[16,4,128,1]{2,3,1,0:T(1,128)S(1)} %bitcast.263, f32[16,4,128,128]{3,2,1,0:T(8,128)} %param.37), kind=kOutput, calls=%fused_computation.235 | convolution fusion | flops 12582912 | bytes 4259840 | tf_op jit(solution)/shard_map/rhd,rhde->rhe/dot_general | solution.py:180
  100.0 6.6 %fusion.36 = f32[16,4,1,128]{3,2,1,0:T(1,128)S(1)} fusion(f32[16,4,128,1]{2,3,1,0:T(1,128)S(1)} %bitcast.262, f32[16,4,128,128]{3,2,1,0:T(8,128)} %param.37, f32[16,4,128,128]{3,2,1,0:T(8,128)S(1)} %copy-done.1, f32[16,4,128]{2,1,0:T(4,128)S(1)} %fusion.104, f32[16,4,128]{2,1,0:T(4,128)S(1)} %get-tuple-element.14, f32[16,4]{1,0:T(8,128)S(1)} %copy.260, ...), kind=kOutput, calls=%fused_computation.61 | convolution fusion | flops 19922944 | bytes 8520208 | tf_op jit(solution)/shard_map/rhd,rhde->rhe/dot_general | solution.py:180
  114.0 7.9 %fusion.30 = f32[16,4,1,128]{3,2,1,0:T(1,128)S(1)} fusion(f32[16,4,128,1]{2,3,1,0:T(1,128)S(1)} %bitcast.272, f32[16,4,128,128]{3,2,1,0:T(8,128)S(1)} %add_select_fusion.6, f32[16,4,128]{2,1,0:T(4,128)S(1)} %fusion.102, f32[16,4,128]{2,1,0:T(4,128)S(1)} %get-tuple-element.16, f32[16,4]{1,0:T(8,128)S(1)} %copy-done.30, f32[16,4]{1,0:T(8,128)S(1)} %copy-done.50, ...), kind=kOutput, calls=%fused_computation.55 | convolution fusion | flops 30408704 | bytes 8651824 | tf_op jit(solution)/shard_map/rhd,rhde->rhe/dot_general | solution.py:180
  122.0 6.4 %add_select_fusion.4 = f32[16,4,128,128]{3,2,1,0:T(8,128)S(1)} fusion(f32[16,4,128]{2,1,0:T(4,128)S(1)} %fusion.101, f32[16,4,128]{2,1,0:T(4,128)S(1)} %get-tuple-element.17, f32[16,4]{1,0:T(8,128)S(1)} %copy-done.32, f32[16,4,128]{2,1,0:T(4,128)S(1)} %fusion.102, f32[16,4,128,128]{3,2,1,0:T(8,128)S(1)} %add_select_fusion.6, ...), kind=kLoop, calls=%fused_computation.17 | loop fusion | flops 26214400 | bytes 12846656 | tf_op jit(solution)/shard_map/jit(_where)/select_n | solution.py:188
  134.2 5.7 %fusion.6 = f32[16,4,128,128]{3,2,1,0:T(8,128)S(1)} fusion(f32[16,4,128]{2,1,0:T(4,128)S(1)} %fusion.101, f32[16,4,128]{2,1,0:T(4,128)S(1)} %get-tuple-element.17, f32[16,4]{1,0:T(8,128)S(1)} %copy-done.32, f32[16,4,128]{2,1,0:T(4,128)S(1)} %fusion.102, f32[16,4,128]{2,1,0:T(4,128)S(1)} %get-tuple-element.16, f32[16,4]{1,0:T(8,128)S(1)} %copy-done.30, ...), kind=kLoop, calls=%fused_computation.19 | loop fusion | flops 20971520 | bytes 8651840 | tf_op jit(solution)/shard_map/jit(_where)/select_n | solution.py:187
  142.0 4.9 %fusion.27 = f32[16,4,1,128]{3,2,1,0:T(1,128)} fusion(f32[16,4,128,1]{2,3,1,0:T(1,128)S(1)} %bitcast.259, f32[16,4,128,128]{3,2,1,0:T(8,128)S(1)} %add_select_fusion.4, f32[16,4,128,128]{3,2,1,0:T(8,128)S(1)} %fusion.6, f32[16,4,128]{2,1,0:T(4,128)S(1)} %fusion.100, f32[16,4,128]{2,1,0:T(4,128)S(1)} %get-tuple-element.18, f32[16,4]{1,0:T(8,128)S(1)} %copy-done.36, ...), kind=kOutput, calls=%fused_computation.52 | convolution fusion | flops 19922944 | bytes 8520208 | tf_op jit(solution)/shard_map/rhd,rhde->rhe/dot_general | solution.py:180
  161.5 111.4 %all-to-all-done.2 = bf16[48,2,128,512]{2,3,1,0:T(8,128)(2,1)} async-done(((bf16[48,2,128,512]{2,3,1,0:T(8,128)(2,1)}), bf16[48,2,128,512]{2,3,1,0:T(8,128)(2,1)}, u32[]{:S(2)}, u32[]{:S(2)}) %all-to-all-start.2) | async-done | bytes 12582944 | tf_op jit(solution)/shard_map/all_to_all | solution.py:121
  272.9 8.6 %fusion.142 = (bf16[48,1,128,512]{2,3,1,0:T(8,128)(2,1)}, bf16[48,1,128,512]{2,3,1,0:T(8,128)(2,1)S(1)}) fusion(bf16[48,2,128,512]{2,3,1,0:T(8,128)(2,1)} %all-to-all-done.2), kind=kLoop, calls=%fused_computation.232 | loop fusion | bytes 25165824 | tf_op jit(solution)/shard_map/slice | solution.py:31
  281.6 4.1 fusion.18
  293.7 4.6 fusion.19
  298.3 5.9 %bitcast_multiply_fusion = f32[48,32,4,128]{3,1,2,0:T(8,128)S(1)} fusion(bf16[48,128,4,128]{1,3,2,0:T(8,128)(2,1)} %bitcast.250, f32[48,4,32,128]{3,2,1,0:T(8,128)S(1)} %copy-done.6, f32[48,32,4]{1,2,0:T(4,128)} %copy.244, f32[48,4,32]{2,1,0:T(4,128)} %get-tuple-element.53, pred[48,128]{1,0:T(8,128)(4,1)} %add_compare_fusion), kind=kOutput, calls=%fused_computation.30 | convolution fusion | flops 206045184 | bytes 12638208 | tf_op jit(solution)/shard_map/shit,sthd->sihd/dot_general | solution.py:42
  304.3 4.7 fusion.10
  325.9 10.3 %add_select_fusion.2 = f32[16,4,128,128]{3,2,1,0:T(8,128)S(1)} fusion(f32[16,4,128]{2,1,0:T(4,128)S(1)} %fusion.99, f32[16,4,128]{2,1,0:T(4,128)S(1)} %copy-done.26, f32[16,4]{1,0:T(8,128)S(1)} %copy.271, f32[16,4,128]{2,1,0:T(4,128)S(1)} %copy-done.22, f32[16,4,128,128]{3,2,1,0:T(8,128)} %copy-done.4, f32[16,4,128]{2,1,0:T(4,128)S(1)} %copy-done.20, ...), kind=kLoop, calls=%fused_computation.11 | loop fusion | flops 36700160 | bytes 12978272 | tf_op jit(solution)/shard_map/jit(_where)/select_n | solution.py:188
  343.3 48.5 %reduce-scatter.3.cloned.1.call-done = bf16[256,1024]{1,0:T(8,128)(2,1)} async-done(((bf16[512,1024]{1,0:T(8,128)(2,1)}), bf16[256,1024]{1,0:T(8,128)(2,1)}) %reduce-scatter.3.cloned.1.call-update) | async-done | bytes 524304 | tf_op jit(solution)/shard_map/reduce_scatter | solution.py:153
  395.0 9.2 %fusion.24 = f32[16,4,1,128]{3,2,1,0:T(1,128)S(1)} fusion(f32[16,4,128,1]{2,3,1,0:T(1,128)} %bitcast.271, f32[16,4,128,128]{3,2,1,0:T(8,128)} %copy-done.5, f32[16,4,128]{2,1,0:T(4,128)} %fusion.98, f32[16,4,128]{2,1,0:T(4,128)} %get-tuple-element.20, f32[16,4]{1,0:T(8,128)} %copy.273, f32[16,4]{1,0:T(8,128)} %copy.253, ...), kind=kOutput, calls=%fused_computation.49 | convolution fusion | flops 30408704 | bytes 8651824 | tf_op jit(solution)/shard_map/rhd,rhde->rhe/dot_general | solution.py:180
  405.6 11.0 %all-gather.2.cloned.1.call-done = bf16[512,1024]{1,0:T(8,128)(2,1)} async-done(((bf16[256,1024]{1,0:T(8,128)(2,1)}), bf16[512,1024]{1,0:T(8,128)(2,1)}) %all-gather.2.cloned.1.call-update) | async-done | bytes 1048592 | tf_op jit(solution)/shard_map/all_gather | solution.py:162
  416.6 5.5 %fusion.14 = f32[512,1408]{1,0:T(8,128)} fusion(bf16[512,1024]{1,0:T(8,128)(2,1)} %all-gather.2.cloned.1.call-done, bf16[2,1024,1408]{2,1,0:T(8,128)(2,1)} %param.42), kind=kOutput, calls=%fused_computation.37 | convolution fusion | flops 1476395008 | bytes 6815744 | tf_op jit(solution)/shard_map/dot_general | solution.py:163
  422.1 7.4 %convolution_convert_fusion = bf16[512,1024]{1,0:T(8,128)(2,1)} fusion(bf16[1408,1024]{1,0:T(8,128)(2,1)S(1)} %copy-done, bf16[512,1024]{1,0:T(8,128)(2,1)} %all-gather.2.cloned.1.call-done, bf16[2,1024,1408]{2,1,0:T(8,128)(2,1)} %param.42, f32[512,1408]{1,0:T(8,128)} %fusion.14), kind=kOutput, calls=%fused_computation.84 | convolution fusion | flops 2957639680 | bytes 10747904 | tf_op jit(solution)/shard_map/dot_general | solution.py:167
  429.6 15.2 %fusion.2 = f32[16,4,128,128]{3,2,1,0:T(8,128)} fusion(f32[16,4,128]{2,1,0:T(4,128)} %fusion.97, f32[16,4,128]{2,1,0:T(4,128)} %get-tuple-element.13, f32[16,4]{1,0:T(8,128)} %copy.275, f32[16,4,128]{2,1,0:T(4,128)} %fusion.98, f32[16,4,128]{2,1,0:T(4,128)} %get-tuple-element.20, f32[16,4]{1,0:T(8,128)} %copy.273, pred[16]{0:T(512)(128)(4,1)} %get-tuple-element.50, ...), kind=kLoop, calls=%fused_computation.7 | loop fusion | flops 41943040 | bytes 8915072 | tf_op jit(solution)/shard_map/jit(_where)/select_n | solution.py:187
  446.1 15.8 %add_select_fusion = f32[16,4,128,128]{3,2,1,0:T(8,128)} fusion(f32[16,4,128]{2,1,0:T(4,128)} %fusion.97, f32[16,4,128]{2,1,0:T(4,128)} %get-tuple-element.13, f32[16,4]{1,0:T(8,128)} %copy.275, f32[16,4,128]{2,1,0:T(4,128)} %fusion.98, f32[16,4,128,128]{3,2,1,0:T(8,128)} %copy-done.5, f32[16,4,128]{2,1,0:T(4,128)} %get-tuple-element.20, f32[16,4]{1,0:T(8,128)} %copy.273, ...), kind=kLoop, calls=%fused_computation.5 | loop fusion | flops 47185920 | bytes 13109888 | tf_op jit(solution)/shard_map/jit(_where)/select_n | solution.py:188
  (242 shorter events, 121.3 us)
Async XLA Ops:
  7.2 414.9 %copy-start = (bf16[1408,1024]{1,0:T(8,128)(2,1)S(1)}, bf16[1408,1024]{1,0:T(8,128)(2,1)}, u32[]{:S(2)}) copy-start(bf16[1408,1024]{1,0:T(8,128)(2,1)} %param.43) | copy-start | bytes 8650756
  8.7 13.7 %all-to-all-start = ((s32[16,3,1]{1,2,0:T(1,128)}), s32[16,3,1]{1,2,0:T(1,128)S(1)}, u32[]{:S(2)}, u32[]{:S(2)}) async-start(s32[16,3,1]{1,2,0:T(1,128)} %bitcast.6), calls=%async_computation | async-start | bytes 16384 | tf_op jit(solution)/shard_map/all_to_all | solution.py:122
  22.4 20.1 %copy-start.48 = (s32[16,3,1]{1,2,0:T(1,128)}, s32[16,3,1]{1,2,0:T(1,128)S(1)}, u32[]{:S(2)}) copy-start(s32[16,3,1]{1,2,0:T(1,128)S(1)} %all-to-all-done) | copy-start | bytes 580
  22.4 20.2 %all-to-all-start.1 = ((s32[16,3,1]{1,2,0:T(1,128)}), s32[16,3,1]{1,2,0:T(1,128)S(1)}, u32[]{:S(2)}, u32[]{:S(2)}) async-start(s32[16,3,1]{1,2,0:T(1,128)} %bitcast.7), calls=%async_computation.1 | async-start | bytes 16384 | tf_op jit(solution)/shard_map/all_to_all | solution.py:123
  43.2 229.8 %all-to-all-start.2 = ((bf16[48,2,128,512]{2,3,1,0:T(8,128)(2,1)}), bf16[48,2,128,512]{2,3,1,0:T(8,128)(2,1)}, u32[]{:S(2)}, u32[]{:S(2)}) async-start(bf16[48,2,128,512]{2,3,1,0:T(8,128)(2,1)} %copy.234), calls=%async_computation.2 | async-start | bytes 25165824 | tf_op jit(solution)/shard_map/all_to_all | solution.py:121
  49.2 342.6 %reduce-scatter.3.cloned.1.call-start = ((), (), s32[]{:S(2)}) async-start(), calls=%async_computation.5 | async-start | bytes 1572864 | tf_op jit(solution)/shard_map/reduce_scatter | solution.py:153
  58.8 11.6 %copy-start.68 = (s32[16,8]{0,1:T(8,128)S(1)}, s32[16,8]{0,1:T(8,128)}, u32[]{:S(2)}) copy-start(s32[16,8]{0,1:T(8,128)} %param.35) | copy-start | bytes 1540
  90.8 9.2 %copy-start.1 = (f32[16,4,128,128]{3,2,1,0:T(8,128)S(1)}, f32[16,4,128,128]{3,2,1,0:T(8,128)}, u32[]{:S(2)}) copy-start(f32[16,4,128,128]{3,2,1,0:T(8,128)} %param.38) | copy-start | bytes 12582916
  90.8 9.2 %copy-start.44 = (f32[16,4]{1,0:T(8,128)S(1)}, f32[16,4]{1,0:T(8,128)}, u32[]{:S(2)}) copy-start(f32[16,4]{1,0:T(8,128)} %copy.259) | copy-start | bytes 772
  92.9 41.3 %copy-start.52 = (pred[16]{0:T(512)(128)(4,1)}, pred[16]{0:T(512)(128)(4,1)S(1)}, u32[]{:S(2)}) copy-start(pred[16]{0:T(512)(128)(4,1)S(1)} %get-tuple-element.52) | copy-start | bytes 52
  92.9 41.3 %copy-start.54 = (pred[16]{0:T(512)(128)(4,1)}, pred[16]{0:T(512)(128)(4,1)S(1)}, u32[]{:S(2)}) copy-start(pred[16]{0:T(512)(128)(4,1)S(1)} %get-tuple-element.46) | copy-start | bytes 52
  92.9 41.3 %copy-start.56 = (pred[16]{0:T(512)(128)(4,1)}, pred[16]{0:T(512)(128)(4,1)S(1)}, u32[]{:S(2)}) copy-start(pred[16]{0:T(512)(128)(4,1)S(1)} %get-tuple-element.47) | copy-start | bytes 52
  92.9 47.1 %copy-start.60 = (pred[16]{0:T(512)(128)(4,1)}, pred[16]{0:T(512)(128)(4,1)S(1)}, u32[]{:S(2)}) copy-start(pred[16]{0:T(512)(128)(4,1)S(1)} %get-tuple-element.48) | copy-start | bytes 52
  94.5 39.7 %copy-start.9 = (f32[16,4,128]{2,1,0:T(4,128)}, f32[16,4,128]{2,1,0:T(4,128)S(1)}, u32[]{:S(2)}) copy-start(f32[16,4,128]{2,1,0:T(4,128)S(1)} %get-tuple-element.16) | copy-start | bytes 98308
  94.5 39.7 %copy-start.11 = (f32[16,4,128]{2,1,0:T(4,128)}, f32[16,4,128]{2,1,0:T(4,128)S(1)}, u32[]{:S(2)}) copy-start(f32[16,4,128]{2,1,0:T(4,128)S(1)} %get-tuple-element.17) | copy-start | bytes 98308
  94.5 45.5 %copy-start.19 = (f32[16,4,128]{2,1,0:T(4,128)}, f32[16,4,128]{2,1,0:T(4,128)S(1)}, u32[]{:S(2)}) copy-start(f32[16,4,128]{2,1,0:T(4,128)S(1)} %get-tuple-element.18) | copy-start | bytes 98308
  113.9 20.2 %copy-start.13 = (f32[16,4,128]{2,1,0:T(4,128)}, f32[16,4,128]{2,1,0:T(4,128)S(1)}, u32[]{:S(2)}) copy-start(f32[16,4,128]{2,1,0:T(4,128)S(1)} %fusion.102) | copy-start | bytes 98308
  122.0 12.2 %copy-start.15 = (f32[16,4,128]{2,1,0:T(4,128)}, f32[16,4,128]{2,1,0:T(4,128)S(1)}, u32[]{:S(2)}) copy-start(f32[16,4,128]{2,1,0:T(4,128)S(1)} %fusion.101) | copy-start | bytes 98308
  128.4 11.6 %copy-start.4 = (f32[16,4,128,128]{3,2,1,0:T(8,128)}, f32[16,4,128,128]{3,2,1,0:T(8,128)S(1)}, u32[]{:S(2)}) copy-start(f32[16,4,128,128]{3,2,1,0:T(8,128)S(1)} %add_select_fusion.4) | copy-start | bytes 12582916
  322.7 93.9 %all-gather.2.cloned.1.call-start = ((), (), s32[]{:S(2)}) async-start(), calls=%async_computation.6 | async-start | bytes 1572864 | tf_op jit(solution)/shard_map/all_gather | solution.py:162
  323.5 12.7 %copy-start.27 = (f32[16,4,128]{2,1,0:T(4,128)}, f32[16,4,128]{2,1,0:T(4,128)S(1)}, u32[]{:S(2)}) copy-start(f32[16,4,128]{2,1,0:T(4,128)S(1)} %fusion.99) | copy-start | bytes 98308
  323.6 12.6 %copy-start.42 = (f32[16,4]{1,0:T(8,128)}, f32[16,4]{1,0:T(8,128)S(1)}, u32[]{:S(2)}) copy-start(f32[16,4]{1,0:T(8,128)S(1)} %copy.271) | copy-start | bytes 772
  325.9 12.4 %copy-start.38 = (f32[16,1,4,128]{3,2,1,0:T(4,128)S(1)}, f32[16,1,4,128]{3,2,1,0:T(4,128)}, u32[]{:S(2)}) copy-start(f32[16,1,4,128]{3,2,1,0:T(4,128)} %get-tuple-element.22) | copy-start | bytes 98308
  395.0 66.9 %reduce-scatter.5.cloned.1.call-start = ((), (), s32[]{:S(2)}) async-start(), calls=%async_computation.7 | async-start | bytes 1572864 | tf_op jit(solution)/shard_map/reduce_scatter | solution.py:166
  (53 other events, 276.1 us)
Sparse Core Ops, SparseCore 0:
  322.8 68.9 reduce-scatter.2
  395.1 21.4 all-gather.1
  429.7 20.3 reduce-scatter.4
where the time goes:
time: 478 us; the launch traced here: 471 us
  waiting for transfers between devices  176 us (37%)
  matrix products  96.6 us (20%)
  other arithmetic  91.4 us (19%)
  local copies, waits for them, and re-layouts  74.8 us (16%)
  starting transfers between devices  17 us (4%)
  between operations  15 us (3%)
    all_to_all x1, waiting for transfers between devices, on_device(): lax.all_to_all(kv_cache, 'req', split_axis=0, concat_axis=0, tiled=True)  111 us
    reduce_scatter x1, waiting for transfers between devices, on_device(): lax.psum_scatter(jnp.dot(mixed, w_out, preferred_element_type=jnp.float32...  48.5 us
    dot_general x8, matrix products, on_device(): jnp.einsum('rhd,rhde->rhe', unit, memory, precision=lax.Precision.HIGHEST)  45.1 us
    select_n x4, other arithmetic, on_device(): memory = jnp.where(live, new_mem, memory)  36 us
    unnamed x143, local copies, waits for them, and re-layouts  21.6 us
    select_n x2, other arithmetic, on_device(): momentum = jnp.where(live, new_mom, momentum)  20.9 us
    all_gather x1, waiting for transfers between devices, on_device(): piece = lax.all_gather(ffn_in, 'grp', axis=0, tiled=True)  11 us
  transfers between devices with their start and end apart: 6, of which 4 were waited for; matrix products, arithmetic and copies ran while one was open for 40% of the time, Pallas kernels for 0%

commit v1 on v0

--- a/solution.py
+++ b/solution.py
@@ -8,6 +8,30 @@
 EPS = 1e-06
 THETA = 0.5
 NEG = -1e30
+
+
+def in_blocks(shard, dim, size):
+    shape = shard.shape
+    blocks = shard.reshape(*shape[:dim], size, shape[dim] // size, *shape[dim + 1 :])
+    return jnp.moveaxis(blocks, dim, 0)
+
+
+def joined_along(pieces, dim):
+    pieces = jnp.moveaxis(pieces, 0, dim)
+    dims = pieces.shape
+    return pieces.reshape(*dims[:dim], dims[dim] * dims[dim + 1], *dims[dim + 2 :])
+
+
+def sent_to_each(x, axis, split_dim, concat_dim):
+    size, index = (lax.axis_size(axis), lax.axis_index(axis))
+    parts = in_blocks(x, split_dim, size)
+    result = parts
+    for turn in range(1, size):
+        target, source = ((index + turn) % size, (index - turn) % size)
+        sent = lax.dynamic_index_in_dim(parts, target, 0)
+        received = lax.ppermute(sent, axis, [(i, (i + turn) % size) for i in range(size)])
+        result = lax.dynamic_update_slice_in_dim(result, received, source, axis=0)
+    return joined_along(result, concat_dim)
 
 
 def rms_norm(rows, gain):
@@ -119,7 +143,7 @@
     request_ids = jnp.arange(reqs, dtype=jnp.int32)
     moved_pages, moved_request, moved_page = (
         lax.all_to_all(kv_cache, "req", split_axis=0, concat_axis=0, tiled=True),
-        lax.all_to_all(slot_request, "req", split_axis=0, concat_axis=0, tiled=True),
+        sent_to_each(slot_request, "req", 0, 0),
         lax.all_to_all(slot_page, "req", split_axis=0, concat_axis=0, tiled=True),
     )
     local_request = moved_request - first_request

time: 478 us -> 514 us (1.075)
  starting transfers between devices: 17 us -> 96.6 us
  waiting for transfers between devices: 176 us -> 115 us
  local copies, waits for them, and re-layouts: 74.8 us -> 91.1 us
    all_to_all x1, waiting for transfers between devices: 111 us -> 0.01 us  [on_device(): lax.all_to_all(kv_cache, 'req', split_axis=0, concat_axis=0, tiled=True)]
    ppermute x0 -> x15, waiting for transfers between devices: none -> 105 us  [sent_to_each(): lax.ppermute(sent, axis, [(i, (i + turn) % size) for i in range(size)])]
    ppermute x0 -> x15, starting transfers between devices: none -> 83.1 us  [sent_to_each(): lax.ppermute(sent, axis, [(i, (i + turn) % size) for i in range(size)])]
    reduce_scatter x1, waiting for transfers between devices: 48.5 us -> 0.01 us  [on_device(): lax.psum_scatter(jnp.dot(mixed, w_out, preferred_element_type=jnp.float32...]
    dynamic_update_slice x0 -> x15, local copies, waits for them, and re-layouts: none -> 19.2 us  [sent_to_each(): result = lax.dynamic_update_slice_in_dim(result, received, source, axis=0)]
    all_to_all x1 -> x0, starting transfers between devices: 7.39 us -> none  [on_device(): lax.all_to_all(slot_request, 'req', split_axis=0, concat_axis=0, tiled=True)]
    unnamed x143 -> x147, local copies, waits for them, and re-layouts: 21.6 us -> 19.6 us
  transfers between devices with their start and end apart: 6 -> 20, of which waited for: 4 -> 2; matrix products, arithmetic and copies ran while one was open for 40% -> 41% of each run, Pallas kernels for 0% -> 0%
where the time goes in v1:
time: 514 us; the launch traced here: 505 us
  waiting for transfers between devices  115 us (22%)
  matrix products  96.7 us (19%)
  starting transfers between devices  96.6 us (19%)
  local copies, waits for them, and re-layouts  91.1 us (18%)
  other arithmetic  90.3 us (18%)
  between operations  15.3 us (3%)
    ppermute x15, waiting for transfers between devices, sent_to_each(): lax.ppermute(sent, axis, [(i, (i + turn) % size) for i in range(size)])  105 us
    ppermute x15, starting transfers between devices, sent_to_each(): lax.ppermute(sent, axis, [(i, (i + turn) % size) for i in range(size)])  83.1 us
    dot_general x8, matrix products, on_device(): jnp.einsum('rhd,rhde->rhe', unit, memory, precision=lax.Precision.HIGHEST)  45.1 us
    select_n x4, other arithmetic, on_device(): memory = jnp.where(live, new_mem, memory)  36 us
    select_n x2, other arithmetic, on_device(): momentum = jnp.where(live, new_mom, momentum)  20.9 us
    unnamed x147, local copies, waits for them, and re-layouts  19.6 us
    dynamic_update_slice x15, local copies, waits for them, and re-layouts, sent_to_each(): result = lax.dynamic_update_slice_in_dim(result, received, source, axis=0)  19.2 us
  transfers between devices with their start and end apart: 20, of which 2 were waited for; matrix products, arithmetic and copies ran while one was open for 41% of the time, Pallas kernels for 0%

profile of v1, /device:TPU:0, one launch (start us, length us, event | category | flops | bytes accessed | tf_op | source)
XLA Modules:
  0.0 505.4 jit_solution(16400865061872435402)
XLA Ops:
  8.7 7.4 %all-to-all-start = ((s32[16,3,1]{1,2,0:T(1,128)}), s32[16,3,1]{1,2,0:T(1,128)S(1)}, u32[]{:S(2)}, u32[]{:S(2)}) async-start(s32[16,3,1]{1,2,0:T(1,128)} %bitcast.6), calls=%async_computation | async-start | bytes 16384 | tf_op jit(solution)/shard_map/all_to_all | solution.py:147
  16.1 16.7 %copy.231 = bf16[48,2,128,512]{2,3,1,0:T(8,128)(2,1)} copy(bf16[48,2,128,512]{3,2,1,0:T(8,128)(2,1)} %param.30) | data formatting | bytes 25165824 | tf_op args[8]
  33.4 6.0 %all-to-all-start.1 = ((bf16[48,2,128,512]{2,3,1,0:T(8,128)(2,1)}), bf16[48,2,128,512]{2,3,1,0:T(8,128)(2,1)}, u32[]{:S(2)}, u32[]{:S(2)}) async-start(bf16[48,2,128,512]{2,3,1,0:T(8,128)(2,1)} %copy.231), calls=%async_computation.1 | async-start | bytes 25165824 | tf_op jit(solution)/shard_map/all_to_all | solution.py:145
  91.7 5.5 %fusion.144 = f32[16,4,1,128]{3,2,1,0:T(1,128)S(1)} fusion(f32[16,4,128,1]{2,3,1,0:T(1,128)S(1)} %bitcast.260, f32[16,4,128,128]{3,2,1,0:T(8,128)} %param.37), kind=kOutput, calls=%fused_computation.249 | convolution fusion | flops 12582912 | bytes 4259840 | tf_op jit(solution)/shard_map/rhd,rhde->rhe/dot_general | solution.py:204
  97.2 6.6 %fusion.36 = f32[16,4,1,128]{3,2,1,0:T(1,128)S(1)} fusion(f32[16,4,128,1]{2,3,1,0:T(1,128)S(1)} %bitcast.259, f32[16,4,128,128]{3,2,1,0:T(8,128)} %param.37, f32[16,4,128,128]{3,2,1,0:T(8,128)S(1)} %copy-done.1, f32[16,4,128]{2,1,0:T(4,128)S(1)} %fusion.104, f32[16,4,128]{2,1,0:T(4,128)S(1)} %get-tuple-element.12, f32[16,4]{1,0:T(8,128)S(1)} %copy.257, ...), kind=kOutput, calls=%fused_computation.61 | convolution fusion | flops 19922944 | bytes 8520208 | tf_op jit(solution)/shard_map/rhd,rhde->rhe/dot_general | solution.py:204
  111.2 7.9 %fusion.30 = f32[16,4,1,128]{3,2,1,0:T(1,128)S(1)} fusion(f32[16,4,128,1]{2,3,1,0:T(1,128)S(1)} %bitcast.269, f32[16,4,128,128]{3,2,1,0:T(8,128)S(1)} %add_select_fusion.6, f32[16,4,128]{2,1,0:T(4,128)S(1)} %fusion.102, f32[16,4,128]{2,1,0:T(4,128)S(1)} %get-tuple-element.14, f32[16,4]{1,0:T(8,128)S(1)} %copy-done.30, f32[16,4]{1,0:T(8,128)S(1)} %copy-done.50, ...), kind=kOutput, calls=%fused_computation.55 | convolution fusion | flops 30408704 | bytes 8651824 | tf_op jit(solution)/shard_map/rhd,rhde->rhe/dot_general | solution.py:204
  119.2 6.4 %add_select_fusion.4 = f32[16,4,128,128]{3,2,1,0:T(8,128)S(1)} fusion(f32[16,4,128]{2,1,0:T(4,128)S(1)} %fusion.101, f32[16,4,128]{2,1,0:T(4,128)S(1)} %get-tuple-element.15, f32[16,4]{1,0:T(8,128)S(1)} %copy-done.32, f32[16,4,128]{2,1,0:T(4,128)S(1)} %fusion.102, f32[16,4,128,128]{3,2,1,0:T(8,128)S(1)} %add_select_fusion.6, ...), kind=kLoop, calls=%fused_computation.17 | loop fusion | flops 26214400 | bytes 12846656 | tf_op jit(solution)/shard_map/jit(_where)/select_n | solution.py:212
  131.5 5.7 %fusion.6 = f32[16,4,128,128]{3,2,1,0:T(8,128)S(1)} fusion(f32[16,4,128]{2,1,0:T(4,128)S(1)} %fusion.101, f32[16,4,128]{2,1,0:T(4,128)S(1)} %get-tuple-element.15, f32[16,4]{1,0:T(8,128)S(1)} %copy-done.32, f32[16,4,128]{2,1,0:T(4,128)S(1)} %fusion.102, f32[16,4,128]{2,1,0:T(4,128)S(1)} %get-tuple-element.14, f32[16,4]{1,0:T(8,128)S(1)} %copy-done.30, ...), kind=kLoop, calls=%fused_computation.19 | loop fusion | flops 20971520 | bytes 8651840 | tf_op jit(solution)/shard_map/jit(_where)/select_n | solution.py:211
  137.3 4.9 fusion.27
  142.2 105.2 %collective-permute-done = s32[1,3]{1,0:T(1,128)} collective-permute-done((s32[1,3]{1,0:T(1,128)}, s32[1,3]{1,0:T(1,128)}, u32[]{:S(2)}, u32[]{:S(2)}) %collective-permute-start) | collective-permute-done | bytes 44 | tf_op jit(solution)/shard_map/ppermute | solution.py:32
  248.7 64.6 %collective-permute-start.6 = (s32[1,3]{1,0:T(1,128)}, s32[1,3]{1,0:T(1,128)}, u32[]{:S(2)}, u32[]{:S(2)}) collective-permute-start(s32[1,3]{1,0:T(1,128)} %get-tuple-element.51), channel_id=1, source_target_pairs={{0,14},{2,16},{4,18},{6,20},{8,22},{10,24},{12,26},{14,28},{16,30}... | collective-permute-start | bytes 44 | tf_op jit(solution)/shard_map/ppermute | solution.py:32
  357.3 8.8 %fusion.141 = (bf16[48,1,128,512]{2,3,1,0:T(8,128)(2,1)}, bf16[48,1,128,512]{2,3,1,0:T(8,128)(2,1)S(1)}) fusion(bf16[48,2,128,512]{2,3,1,0:T(8,128)(2,1)} %all-to-all-done.1), kind=kLoop, calls=%fused_computation.246 | loop fusion | bytes 25165824 | tf_op jit(solution)/shard_map/slice | solution.py:55
  366.1 4.1 fusion.18
  378.3 4.1 fusion.19
  382.4 5.9 %bitcast_multiply_fusion = f32[48,32,4,128]{3,1,2,0:T(8,128)S(1)} fusion(bf16[48,128,4,128]{1,3,2,0:T(8,128)(2,1)} %bitcast.247, f32[48,4,32,128]{3,2,1,0:T(8,128)S(1)} %copy-done.6, f32[48,32,4]{1,2,0:T(4,128)} %copy.241, f32[48,4,32]{2,1,0:T(4,128)} %get-tuple-element.66, pred[48,128]{1,0:T(8,128)(4,1)} %add_compare_fusion), kind=kOutput, calls=%fused_computation.30 | convolution fusion | flops 206045184 | bytes 12638208 | tf_op jit(solution)/shard_map/shit,sthd->sihd/dot_general | solution.py:66
  388.3 4.7 fusion.10
  400.4 3.9 fusion.70
  410.0 10.3 %add_select_fusion.2 = f32[16,4,128,128]{3,2,1,0:T(8,128)S(1)} fusion(f32[16,4,128]{2,1,0:T(4,128)S(1)} %fusion.99, f32[16,4,128]{2,1,0:T(4,128)S(1)} %copy-done.26, f32[16,4]{1,0:T(8,128)S(1)} %copy.268, f32[16,4,128]{2,1,0:T(4,128)S(1)} %copy-done.22, f32[16,4,128,128]{3,2,1,0:T(8,128)} %copy-done.4, f32[16,4,128]{2,1,0:T(4,128)S(1)} %copy-done.20, ...), kind=kLoop, calls=%fused_computation.11 | loop fusion | flops 36700160 | bytes 12978272 | tf_op jit(solution)/shard_map/jit(_where)/select_n | solution.py:212
  430.6 9.2 %fusion.24 = f32[16,4,1,128]{3,2,1,0:T(1,128)S(1)} fusion(f32[16,4,128,1]{2,3,1,0:T(1,128)} %bitcast.268, f32[16,4,128,128]{3,2,1,0:T(8,128)} %copy-done.5, f32[16,4,128]{2,1,0:T(4,128)} %fusion.98, f32[16,4,128]{2,1,0:T(4,128)} %get-tuple-element.18, f32[16,4]{1,0:T(8,128)} %copy.270, f32[16,4]{1,0:T(8,128)} %copy.250, ...), kind=kOutput, calls=%fused_computation.49 | convolution fusion | flops 30408704 | bytes 8651824 | tf_op jit(solution)/shard_map/rhd,rhde->rhe/dot_general | solution.py:204
  441.2 10.0 %all-gather.2.cloned.1.call-done = bf16[512,1024]{1,0:T(8,128)(2,1)} async-done(((bf16[256,1024]{1,0:T(8,128)(2,1)}), bf16[512,1024]{1,0:T(8,128)(2,1)}) %all-gather.2.cloned.1.call-update) | async-done | bytes 1048592 | tf_op jit(solution)/shard_map/all_gather | solution.py:186
  451.3 5.5 %fusion.14 = f32[512,1408]{1,0:T(8,128)} fusion(bf16[512,1024]{1,0:T(8,128)(2,1)} %all-gather.2.cloned.1.call-done, bf16[2,1024,1408]{2,1,0:T(8,128)(2,1)} %param.42), kind=kOutput, calls=%fused_computation.37 | convolution fusion | flops 1476395008 | bytes 6815744 | tf_op jit(solution)/shard_map/dot_general | solution.py:187
  456.8 7.5 %convolution_convert_fusion = bf16[512,1024]{1,0:T(8,128)(2,1)} fusion(bf16[1408,1024]{1,0:T(8,128)(2,1)S(1)} %copy-done, bf16[512,1024]{1,0:T(8,128)(2,1)} %all-gather.2.cloned.1.call-done, bf16[2,1024,1408]{2,1,0:T(8,128)(2,1)} %param.42, f32[512,1408]{1,0:T(8,128)} %fusion.14), kind=kOutput, calls=%fused_computation.84 | convolution fusion | flops 2957639680 | bytes 10747904 | tf_op jit(solution)/shard_map/dot_general | solution.py:191
  464.3 15.2 %fusion.2 = f32[16,4,128,128]{3,2,1,0:T(8,128)} fusion(f32[16,4,128]{2,1,0:T(4,128)} %fusion.97, f32[16,4,128]{2,1,0:T(4,128)} %get-tuple-element.11, f32[16,4]{1,0:T(8,128)} %copy.272, f32[16,4,128]{2,1,0:T(4,128)} %fusion.98, f32[16,4,128]{2,1,0:T(4,128)} %get-tuple-element.18, f32[16,4]{1,0:T(8,128)} %copy.270, pred[16]{0:T(512)(128)(4,1)} %get-tuple-element.63, ...), kind=kLoop, calls=%fused_computation.7 | loop fusion | flops 41943040 | bytes 8915072 | tf_op jit(solution)/shard_map/jit(_where)/select_n | solution.py:211
  480.8 15.8 %add_select_fusion = f32[16,4,128,128]{3,2,1,0:T(8,128)} fusion(f32[16,4,128]{2,1,0:T(4,128)} %fusion.97, f32[16,4,128]{2,1,0:T(4,128)} %get-tuple-element.11, f32[16,4]{1,0:T(8,128)} %copy.272, f32[16,4,128]{2,1,0:T(4,128)} %fusion.98, f32[16,4,128,128]{3,2,1,0:T(8,128)} %copy-done.5, f32[16,4,128]{2,1,0:T(4,128)} %get-tuple-element.18, f32[16,4]{1,0:T(8,128)} %copy.270, ...), kind=kLoop, calls=%fused_computation.5 | loop fusion | flops 47185920 | bytes 13109888 | tf_op jit(solution)/shard_map/jit(_where)/select_n | solution.py:212
  (289 shorter events, 148.0 us)
Async XLA Ops:
  7.2 449.6 %copy-start = (bf16[1408,1024]{1,0:T(8,128)(2,1)S(1)}, bf16[1408,1024]{1,0:T(8,128)(2,1)}, u32[]{:S(2)}) copy-start(bf16[1408,1024]{1,0:T(8,128)(2,1)} %param.43) | copy-start | bytes 8650756
  8.7 24.1 %all-to-all-start = ((s32[16,3,1]{1,2,0:T(1,128)}), s32[16,3,1]{1,2,0:T(1,128)S(1)}, u32[]{:S(2)}, u32[]{:S(2)}) async-start(s32[16,3,1]{1,2,0:T(1,128)} %bitcast.6), calls=%async_computation | async-start | bytes 16384 | tf_op jit(solution)/shard_map/all_to_all | solution.py:147
  33.4 323.9 %all-to-all-start.1 = ((bf16[48,2,128,512]{2,3,1,0:T(8,128)(2,1)}), bf16[48,2,128,512]{2,3,1,0:T(8,128)(2,1)}, u32[]{:S(2)}, u32[]{:S(2)}) async-start(bf16[48,2,128,512]{2,3,1,0:T(8,128)(2,1)} %copy.231), calls=%async_computation.1 | async-start | bytes 25165824 | tf_op jit(solution)/shard_map/all_to_all | solution.py:145
  39.4 388.0 %reduce-scatter.3.cloned.1.call-start = ((), (), s32[]{:S(2)}) async-start(), calls=%async_computation.4 | async-start | bytes 1572864 | tf_op jit(solution)/shard_map/reduce_scatter | solution.py:177
  40.5 206.9 %collective-permute-start = (s32[1,3]{1,0:T(1,128)}, s32[1,3]{1,0:T(1,128)}, u32[]{:S(2)}, u32[]{:S(2)}) collective-permute-start(s32[1,3]{1,0:T(1,128)} %get-tuple-element.57), channel_id=1, source_target_pairs={{0,2},{2,4},{4,6},{6,8},{8,10},{10,12},{12,14},{14,16},{16,18},{18... | collective-permute-start | bytes 44 | tf_op jit(solution)/shard_map/ppermute | solution.py:32
  40.9 207.7 %collective-permute-start.1 = (s32[1,3]{1,0:T(1,128)}, s32[1,3]{1,0:T(1,128)}, u32[]{:S(2)}, u32[]{:S(2)}) collective-permute-start(s32[1,3]{1,0:T(1,128)} %get-tuple-element.56), channel_id=1, source_target_pairs={{0,4},{2,6},{4,8},{6,10},{8,12},{10,14},{12,16},{14,18},{16,20},{1... | collective-permute-start | bytes 44 | tf_op jit(solution)/shard_map/ppermute | solution.py:32
  42.6 272.0 %collective-permute-start.2 = (s32[1,3]{1,0:T(1,128)}, s32[1,3]{1,0:T(1,128)}, u32[]{:S(2)}, u32[]{:S(2)}) collective-permute-start(s32[1,3]{1,0:T(1,128)} %get-tuple-element.55), channel_id=1, source_target_pairs={{0,6},{2,8},{4,10},{6,12},{8,14},{10,16},{12,18},{14,20},{16,22},{... | collective-permute-start | bytes 44 | tf_op jit(solution)/shard_map/ppermute | solution.py:32
  44.8 273.2 %collective-permute-start.3 = (s32[1,3]{1,0:T(1,128)}, s32[1,3]{1,0:T(1,128)}, u32[]{:S(2)}, u32[]{:S(2)}) collective-permute-start(s32[1,3]{1,0:T(1,128)} %get-tuple-element.54), channel_id=1, source_target_pairs={{0,8},{2,10},{4,12},{6,14},{8,16},{10,18},{12,20},{14,22},{16,24},... | collective-permute-start | bytes 44 | tf_op jit(solution)/shard_map/ppermute | solution.py:32
  46.3 275.4 %collective-permute-start.4 = (s32[1,3]{1,0:T(1,128)}, s32[1,3]{1,0:T(1,128)}, u32[]{:S(2)}, u32[]{:S(2)}) collective-permute-start(s32[1,3]{1,0:T(1,128)} %get-tuple-element.53), channel_id=1, source_target_pairs={{0,10},{2,12},{4,14},{6,16},{8,18},{10,20},{12,22},{14,24},{16,26}... | collective-permute-start | bytes 44 | tf_op jit(solution)/shard_map/ppermute | solution.py:32
  90.1 47.1 %copy-start.60 = (pred[16]{0:T(512)(128)(4,1)}, pred[16]{0:T(512)(128)(4,1)S(1)}, u32[]{:S(2)}) copy-start(pred[16]{0:T(512)(128)(4,1)S(1)} %get-tuple-element.61) | copy-start | bytes 52
  91.7 45.5 %copy-start.19 = (f32[16,4,128]{2,1,0:T(4,128)}, f32[16,4,128]{2,1,0:T(4,128)S(1)}, u32[]{:S(2)}) copy-start(f32[16,4,128]{2,1,0:T(4,128)S(1)} %get-tuple-element.16) | copy-start | bytes 98308
  137.3 197.3 %copy-start.70 = (s32[1,3]{1,0:T(1,128)S(1)}, s32[1,3]{1,0:T(1,128)}, u32[]{:S(2)}) copy-start(s32[1,3]{1,0:T(1,128)} %get-tuple-element.43) | copy-start | bytes 40
  247.4 79.4 %collective-permute-start.5 = (s32[1,3]{1,0:T(1,128)}, s32[1,3]{1,0:T(1,128)}, u32[]{:S(2)}, u32[]{:S(2)}) collective-permute-start(s32[1,3]{1,0:T(1,128)} %get-tuple-element.52), channel_id=1, source_target_pairs={{0,12},{2,14},{4,16},{6,18},{8,20},{10,22},{12,24},{14,26},{16,28}... | collective-permute-start | bytes 44 | tf_op jit(solution)/shard_map/ppermute | solution.py:32
  248.7 79.4 %collective-permute-start.6 = (s32[1,3]{1,0:T(1,128)}, s32[1,3]{1,0:T(1,128)}, u32[]{:S(2)}, u32[]{:S(2)}) collective-permute-start(s32[1,3]{1,0:T(1,128)} %get-tuple-element.51), channel_id=1, source_target_pairs={{0,14},{2,16},{4,18},{6,20},{8,22},{10,24},{12,26},{14,28},{16,30}... | collective-permute-start | bytes 44 | tf_op jit(solution)/shard_map/ppermute | solution.py:32
  314.6 17.2 %collective-permute-start.7 = (s32[1,3]{1,0:T(1,128)}, s32[1,3]{1,0:T(1,128)}, u32[]{:S(2)}, u32[]{:S(2)}) collective-permute-start(s32[1,3]{1,0:T(1,128)} %get-tuple-element.50), channel_id=1, source_target_pairs={{0,16},{2,18},{4,20},{6,22},{8,24},{10,26},{12,28},{14,30},{16,0},... | collective-permute-start | bytes 44 | tf_op jit(solution)/shard_map/ppermute | solution.py:32
  318.1 15.0 %collective-permute-start.8 = (s32[1,3]{1,0:T(1,128)}, s32[1,3]{1,0:T(1,128)}, u32[]{:S(2)}, u32[]{:S(2)}) collective-permute-start(s32[1,3]{1,0:T(1,128)} %get-tuple-element.49), channel_id=1, source_target_pairs={{0,18},{2,20},{4,22},{6,24},{8,26},{10,28},{12,30},{14,0},{16,2},{... | collective-permute-start | bytes 44 | tf_op jit(solution)/shard_map/ppermute | solution.py:32
  321.7 12.9 %collective-permute-start.9 = (s32[1,3]{1,0:T(1,128)}, s32[1,3]{1,0:T(1,128)}, u32[]{:S(2)}, u32[]{:S(2)}) collective-permute-start(s32[1,3]{1,0:T(1,128)} %get-tuple-element.48), channel_id=1, source_target_pairs={{0,20},{2,22},{4,24},{6,26},{8,28},{10,30},{12,0},{14,2},{16,4},{1... | collective-permute-start | bytes 44 | tf_op jit(solution)/shard_map/ppermute | solution.py:32
  326.8 10.6 %collective-permute-start.10 = (s32[1,3]{1,0:T(1,128)}, s32[1,3]{1,0:T(1,128)}, u32[]{:S(2)}, u32[]{:S(2)}) collective-permute-start(s32[1,3]{1,0:T(1,128)} %get-tuple-element.47), channel_id=1, source_target_pairs={{0,22},{2,24},{4,26},{6,28},{8,30},{10,0},{12,2},{14,4},{16,6},{18... | collective-permute-start | bytes 44 | tf_op jit(solution)/shard_map/ppermute | solution.py:32
  328.1 10.6 %collective-permute-start.11 = (s32[1,3]{1,0:T(1,128)}, s32[1,3]{1,0:T(1,128)}, u32[]{:S(2)}, u32[]{:S(2)}) collective-permute-start(s32[1,3]{1,0:T(1,128)} %get-tuple-element.46), channel_id=1, source_target_pairs={{0,24},{2,26},{4,28},{6,30},{8,0},{10,2},{12,4},{14,6},{16,8},{18,... | collective-permute-start | bytes 44 | tf_op jit(solution)/shard_map/ppermute | solution.py:32
  331.7 8.2 %collective-permute-start.12 = (s32[1,3]{1,0:T(1,128)}, s32[1,3]{1,0:T(1,128)}, u32[]{:S(2)}, u32[]{:S(2)}) collective-permute-start(s32[1,3]{1,0:T(1,128)} %get-tuple-element.45), channel_id=1, source_target_pairs={{0,26},{2,28},{4,30},{6,0},{8,2},{10,4},{12,6},{14,8},{16,10},{18,... | collective-permute-start | bytes 44 | tf_op jit(solution)/shard_map/ppermute | solution.py:32
  333.0 8.2 %collective-permute-start.13 = (s32[1,3]{1,0:T(1,128)}, s32[1,3]{1,0:T(1,128)}, u32[]{:S(2)}, u32[]{:S(2)}) collective-permute-start(s32[1,3]{1,0:T(1,128)} %get-tuple-element.44), channel_id=1, source_target_pairs={{0,28},{2,30},{4,0},{6,2},{8,4},{10,6},{12,8},{14,10},{16,12},{18,... | collective-permute-start | bytes 44 | tf_op jit(solution)/shard_map/ppermute | solution.py:32
  334.6 7.9 %collective-permute-start.14 = (s32[1,3]{1,0:T(1,128)S(1)}, s32[1,3]{1,0:T(1,128)}, u32[]{:S(2)}, u32[]{:S(2)}) collective-permute-start(s32[1,3]{1,0:T(1,128)S(1)} %copy-done.70), channel_id=1, source_target_pairs={{0,30},{2,0},{4,2},{6,4},{8,6},{10,8},{12,10},{14,12},{16,14},{18,... | collective-permute-start | bytes 44 | tf_op jit(solution)/shard_map/ppermute | solution.py:32
  406.8 44.5 %all-gather.2.cloned.1.call-start = ((), (), s32[]{:S(2)}) async-start(), calls=%async_computation.5 | async-start | bytes 1572864 | tf_op jit(solution)/shard_map/all_gather | solution.py:186
  430.6 66.0 %reduce-scatter.5.cloned.1.call-start = ((), (), s32[]{:S(2)}) async-start(), calls=%async_computation.6 | async-start | bytes 1572864 | tf_op jit(solution)/shard_map/reduce_scatter | solution.py:190
  (69 other events, 627.6 us)
Sparse Core Ops, SparseCore 0:
  406.9 19.5 reduce-scatter.2
  430.7 20.5 all-gather.1
  464.4 20.3 reduce-scatter.4
